TPU v7x, 512 devices: a whole 4x8x8 slice. The times are simulated.
512 devices in a mesh: tp: 64 (over y, z_hi, core), ep: 8 (over x, z_lo).
Axes of the slice: x: 4, y: 8, z: 8 (z_hi: 4, z_lo: 2; z = z_hi * 2 + z_lo), core: 2. Of those that a mesh axis runs over, the one named last changes fastest.
Arguments:
- residual: bfloat16 [8, 7168, 256], P('ep', 'tp')
- out_grad: bfloat16 [8, 7168, 256], P('ep', 'tp'), may hold values from -6 to 6
- norm_gain: float32 [7168], P('tp'), may hold values from 0.25 to 1.75
- context: bfloat16 [8, 16384, 256], P('ep', 'tp'), may hold values from -0.3125 to 0.3125
- w_out: bfloat16 [7168, 16384], P('ep', 'tp'), may hold values from -0.046875 to 0.046875
- w_gate: bfloat16 [8, 7168, 2048], P('ep', 'tp'), may hold values from -0.0625 to 0.0625
- w_up: bfloat16 [8, 7168, 2048], P('ep', 'tp'), may hold values from -0.0625 to 0.0625
- w_down: bfloat16 [8, 7168, 2048], P('ep', 'tp'), may hold values from -0.125 to 0.125
- slot_token: int32 [8, 8, 8], P('ep'), may hold values from 0 to 255, as said below
- slot_count: int32 [8, 8], P('ep'), may hold values from 1 to 8, as said below
- slot_gate: float32 [8, 8, 8], P('ep'), may hold values from 0.25 to 2.5
Outputs:
- resid_grad: bfloat16 [8, 7168, 256], P('ep', 'tp')
- context_grad: bfloat16 [8, 16384, 256], P('ep', 'tp')
- w_out_grad: bfloat16 [7168, 16384], P('ep', 'tp')
- gate_grad: bfloat16 [8, 7168, 2048], P('ep', 'tp')
- up_grad: bfloat16 [8, 7168, 2048], P('ep', 'tp')
- down_grad: bfloat16 [8, 7168, 2048], P('ep', 'tp')
Inputs may be any that keep to these rules, and one draw needn't show every extreme that they name: `slot_token`: within one group and expert the 8 token positions are distinct; slots at or beyond slot_count are unused. `slot_count`: in every draw one expert has 8 tokens from every group.
All inputs are finite; a program needn't handle non-finite values.
Results may differ from a plain program's by a relative error of at most 0.014.
Values may be sent and summed in bfloat16 or wider, within the bound.
A program may use at most 64 MiB of HBM per device.

v0:
```python
import jax
import jax.numpy as jnp
from jax import lax
from jax.sharding import PartitionSpec as P

norm_eps = 1e-06


def contract_rows(left, right):
    return lax.dot_general(
        left, right, (((0,), (0,)), ((), ())), preferred_element_type=jnp.float32
    )


def contract_cols(left, right):
    return lax.dot_general(
        left, right, (((1,), (1,)), ((), ())), preferred_element_type=jnp.float32
    )


def activate(pre_gate, pre_up, hid_grad):
    sigmoid_gate = jax.nn.sigmoid(pre_gate)
    silu_gate = pre_gate * sigmoid_gate
    hidden = (silu_gate * pre_up).astype(jnp.bfloat16)
    d_gate = (hid_grad * pre_up * sigmoid_gate * (1.0 + pre_gate * (1.0 - sigmoid_gate))).astype(
        jnp.bfloat16
    )
    d_up = (hid_grad * silu_gate).astype(jnp.bfloat16)
    return (hidden, d_gate, d_up)


def shards(
    residual,
    out_grad,
    norm_gain,
    context,
    w_out,
    w_gate,
    w_up,
    w_down,
    slot_token,
    slot_count,
    slot_gate,
):
    tp_count = lax.axis_size("tp")
    stream = residual[0].astype(jnp.float32)
    grad_in = out_grad[0].astype(jnp.float32)
    feat_share, group_rows = stream.shape
    features = feat_share * tp_count
    square = lax.psum(jnp.sum(stream * stream, axis=0), "tp")
    inv_rms = lax.rsqrt(square / features + norm_eps)[None, :]
    normed = stream * inv_rms
    gain_col = norm_gain[:, None]
    inputs = (normed * gain_col).astype(jnp.bfloat16)
    slot_table = slot_token[0]
    capacity = slot_table.shape[1]
    live_mask = jnp.arange(capacity)[None, :] < slot_count[0][:, None]
    one_hot = (
        (slot_table[:, :, None] == jnp.arange(group_rows)[None, None, :]) & live_mask[:, :, None]
    ).astype(jnp.bfloat16)
    send_x = jnp.einsum("dt,ect->edc", inputs, one_hot, preferred_element_type=jnp.float32).astype(
        jnp.bfloat16
    )
    go_rows = jnp.einsum("dt,ect->edc", out_grad[0], one_hot, preferred_element_type=jnp.float32)
    send_go = (slot_gate[0][:, None, :] * go_rows).astype(jnp.bfloat16)
    recv_x, recv_go = (
        lax.all_to_all(send_x, "ep", split_axis=0, concat_axis=2, tiled=True),
        lax.all_to_all(send_go, "ep", split_axis=0, concat_axis=2, tiled=True),
    )
    rows_x = recv_x[0]
    rows_go = recv_go[0]
    gate_w = w_gate[0]
    up_w = w_up[0]
    down_w = w_down[0]
    gate_part = contract_rows(rows_x, gate_w)
    up_part = contract_rows(rows_x, up_w)
    hid_part = contract_rows(rows_go, down_w)
    pre_gate, pre_up, hid_grad = lax.psum((gate_part, up_part, hid_part), "tp")
    hidden, d_gate, d_up = activate(pre_gate, pre_up, hid_grad)
    down_grad = jnp.dot(rows_go, hidden, preferred_element_type=jnp.float32).astype(jnp.bfloat16)[
        None
    ]
    gate_grad = jnp.dot(rows_x, d_gate, preferred_element_type=jnp.float32).astype(jnp.bfloat16)[
        None
    ]
    up_grad = jnp.dot(rows_x, d_up, preferred_element_type=jnp.float32).astype(jnp.bfloat16)[None]
    slot_back = (contract_cols(gate_w, d_gate) + contract_cols(up_w, d_up)).astype(jnp.bfloat16)
    returned = lax.all_to_all(slot_back[None], "ep", split_axis=2, concat_axis=0, tiled=True)
    in_grad = jnp.einsum(
        "edc,ect->dt", returned, one_hot, preferred_element_type=jnp.float32
    ).astype(jnp.bfloat16)
    scaled = in_grad.astype(jnp.float32) * gain_col
    dots = lax.psum(jnp.sum(scaled * normed, axis=0), "tp")
    resid = (grad_in + inv_rms * (scaled - normed * (dots / features)[None, :])).astype(
        jnp.bfloat16
    )
    full_grad = lax.all_gather(resid, "tp", axis=0, tiled=True)
    grad_block = lax.all_to_all(full_grad, "ep", split_axis=0, concat_axis=1, tiled=True)
    ctx_local = context[0]
    ctx_all = lax.all_gather(ctx_local, "ep", axis=1, tiled=True)
    weight_sum = contract_cols(grad_block, ctx_all)
    ctx_total = contract_rows(lax.all_gather(w_out, "ep", axis=0, tiled=True), full_grad)
    return (
        resid[None],
        ctx_total.astype(jnp.bfloat16)[None],
        weight_sum.astype(jnp.bfloat16),
        gate_grad,
        up_grad,
        down_grad,
    )


def solution(mesh):
    return jax.shard_map(
        shards,
        mesh=mesh,
        in_specs=(
            P("ep", "tp", None),
            P("ep", "tp", None),
            P("tp"),
            P("ep", "tp", None),
            P("ep", "tp"),
            P("ep", "tp", None),
            P("ep", "tp", None),
            P("ep", "tp", None),
            P("ep", None, None),
            P("ep", None),
            P("ep", None, None),
        ),
        out_specs=(
            P("ep", "tp", None),
            P("ep", "tp", None),
            P("ep", "tp"),
            P("ep", "tp", None),
            P("ep", "tp", None),
            P("ep", "tp", None),
        ),
        check_vma=False,
    )
```

profile of v0, /device:TPU:2, one launch (start us, length us, event | category | flops | bytes accessed | tf_op | source)
XLA Modules:
  0.0 1152.4 jit_solution(9309882180991946875)
XLA Ops:
  7.2 0.0 copy-start
  7.2 0.9 fusion.32
  8.1 150.2 %psum.35 = f32[256]{0:T(256)S(1)} all-reduce(f32[256]{0:T(256)S(1)} %fusion.32), channel_id=1, replica_groups=mesh['tp'=64,'ep'=8] {'tp'}, use_global_device_ids=true, to_apply=%region_1.0 | all-reduce | flops 256 | bytes 2048 | tf_op jit(solution)/shard_map/psum | solution.py:50
  158.3 0.7 iota_compare_fusion.1
  159.1 1.6 fusion.9
  160.7 5.7 all-to-all-start.1
  166.5 1.6 fusion.11
  168.1 3.1 all-to-all-done.1
  171.2 4.7 all-to-all-start
  175.9 0.0 all-reduce.3.cloned.1.call-start
  175.9 0.0 copy-done
  175.9 1.0 fusion.16
  177.0 2.1 fusion.19
  179.1 1.7 all-to-all-done
  180.7 2.0 fusion.21
  182.8 0.0 all-reduce.3.cloned.1.call-update
  182.8 0.0 all-gather.5.cloned.1.call-start
  182.8 554.5 %all-reduce.3.cloned.1.call-done = (f32[64,2048]{1,0:T(8,128)}, f32[64,2048]{1,0:T(8,128)}, f32[64,2048]{1,0:T(8,128)}) async-done(((f32[64,2048]{1,0:T(8,128)}, f32[64,2048]{1,0:T(8,128)}, f32[64,2048]{1,0:T(8,128)}), (f32[64,2048]{1,0:T(8,128)}, f32[64,2048]{1,0:T(8,128)}, f32[64,2048]{1,0:T(8,128)})) %all-reduce.3.cloned.1.call-update) | async-done | bytes 1572880 | tf_op jit(solution)/shard_map/psum | solution.py:78
  737.3 1.6 multiply_convert_fusion.1
  738.9 0.3 fusion.14
  739.2 0.0 copy-done.1
  739.3 0.3 fusion.10
  739.6 0.5 broadcast.36
  740.1 0.7 reduce
  740.8 0.1 reshape.53
  740.9 9.5 all_to_all.67
  750.5 0.1 reshape.54
  750.6 0.0 copy-done.4
  750.6 0.3 fusion.27
  750.9 142.3 %psum.39 = f32[256]{0:T(256)S(1)} all-reduce(f32[256]{0:T(256)S(1)} %get-tuple-element.35), channel_id=1, replica_groups=mesh['tp'=64,'ep'=8] {'tp'}, use_global_device_ids=true, to_apply=%region_6.0 | all-reduce | flops 256 | bytes 2048 | tf_op jit(solution)/shard_map/psum | solution.py:93
  893.2 0.7 fusion.31
  893.9 0.0 all-gather.5.cloned.1.call-update
  893.9 0.0 all-gather.7.cloned.1.call-start
  893.9 0.7 all-gather.7.cloned.1.call-update
  894.6 78.9 %all-gather.5.cloned.1.call-done = bf16[7168,256]{1,0:T(8,128)(2,1)} async-done(((bf16[112,256]{1,0:T(8,128)(2,1)}), bf16[7168,256]{1,0:T(8,128)(2,1)}) %all-gather.5.cloned.1.call-update) | async-done | bytes 3670032 | tf_op jit(solution)/shard_map/all_gather | solution.py:97
  973.5 6.2 copy.32
  979.8 6.5 all-to-all-start.3
  986.3 0.6 all-gather.9.cloned.1.call-update
  986.9 1.1 fusion
  987.9 1.1 fusion.1
  989.0 0.0 copy-done.3
  989.0 1.1 fusion.2
  990.1 107.2 %all-gather.7.cloned.1.call-done = bf16[7168,256]{1,0:T(8,128)(2,1)} async-done(((bf16[896,256]{1,0:T(8,128)(2,1)}), bf16[7168,256]{1,0:T(8,128)(2,1)}) %all-gather.7.cloned.1.call-update) | async-done | bytes 3670032 | tf_op jit(solution)/shard_map/all_gather | solution.py:102
  1097.3 4.3 fusion.3
  1101.6 0.8 copy.33
  1102.4 39.3 %all-gather.9.cloned.1.call-done = bf16[1,256,2048]{2,1,0:T(8,128)(2,1)} async-done(((bf16[1,256,256]{2,1,0:T(8,128)(2,1)}), bf16[1,256,2048]{2,1,0:T(8,128)(2,1)}) %all-gather.9.cloned.1.call-update) | async-done | bytes 1048592 | tf_op jit(solution)/shard_map/all_gather | solution.py:100
  1141.6 0.0 all-to-all-done.3
  1141.6 4.3 convolution_convert_fusion.3
  (15 shorter events, 0.1 us)
Async XLA Ops:
  7.2 168.8 %copy-start = (bf16[1,112,2048]{2,1,0:T(8,128)(2,1)S(1)}, bf16[1,112,2048]{2,1,0:T(8,128)(2,1)}, u32[]{:S(2)}) copy-start(bf16[1,112,2048]{2,1,0:T(8,128)(2,1)} %param.16) | copy-start | bytes 1376260
  160.7 10.5 all-to-all-start.1
  171.2 9.5 all-to-all-start
  175.9 563.3 %copy-start.1 = (bf16[1,112,2048]{2,1,0:T(8,128)(2,1)S(1)}, bf16[1,112,2048]{2,1,0:T(8,128)(2,1)}, u32[]{:S(2)}) copy-start(bf16[1,112,2048]{2,1,0:T(8,128)(2,1)} %param.17) | copy-start | bytes 1376260
  175.9 561.4 %all-reduce.3.cloned.1.call-start = ((), (), s32[]{:S(2)}) async-start(), calls=%async_computation.7 | async-start | bytes 3145728 | tf_op jit(solution)/shard_map/psum | solution.py:78
  176.9 573.6 %copy-start.4 = (bf16[1,112,256]{2,1,0:T(8,128)(2,1)S(1)}, bf16[1,112,256]{2,1,0:T(8,128)(2,1)}, u32[]{:S(2)}) copy-start(bf16[1,112,256]{2,1,0:T(8,128)(2,1)} %param.11) | copy-start | bytes 172036
  176.9 573.6 %copy-start.6 = (s32[1,8,8]{2,1,0:T(8,128)S(1)}, s32[1,8,8]{2,1,0:T(8,128)}, u32[]{:S(2)}) copy-start(s32[1,8,8]{2,1,0:T(8,128)} %param.19) | copy-start | bytes 772
  177.0 573.6 %copy-start.7 = (f32[112]{0:T(128)S(1)}, f32[112]{0:T(128)}, u32[]{:S(2)}) copy-start(f32[112]{0:T(128)} %param.13) | copy-start | bytes 1348
  177.0 716.3 %copy-start.5 = (bf16[1,112,256]{2,1,0:T(8,128)(2,1)S(1)}, bf16[1,112,256]{2,1,0:T(8,128)(2,1)}, u32[]{:S(2)}) copy-start(bf16[1,112,256]{2,1,0:T(8,128)(2,1)} %param.12) | copy-start | bytes 172036
  182.8 790.7 %all-gather.5.cloned.1.call-start = ((), (), s32[]{:S(2)}) async-start(), calls=%async_computation.4 | async-start | bytes 3727360 | tf_op jit(solution)/shard_map/all_gather | solution.py:97
  893.9 203.4 %all-gather.7.cloned.1.call-start = ((), (), s32[]{:S(2)}) async-start(), calls=%async_computation.5 | async-start | bytes 4128768 | tf_op jit(solution)/shard_map/all_gather | solution.py:102
  979.8 9.3 copy-start.2
  979.8 9.3 copy-start.3
  979.8 161.9 %all-to-all-start.3 = ((bf16[8,896,256]{1,2,0:T(8,128)(2,1)}), bf16[8,896,256]{1,2,0:T(8,128)(2,1)}, u32[]{:S(2)}, u32[]{:S(2)}) async-start(bf16[8,896,256]{1,2,0:T(8,128)(2,1)} %copy.32), calls=%async_computation.3 | async-start | bytes 7340032 | tf_op jit(solution)/shard_map/all_to_all | solution.py:98
  986.3 155.3 %all-gather.9.cloned.1.call-start = ((), (), s32[]{:S(2)}) async-start(), calls=%async_computation.6 | async-start | bytes 1179648 | tf_op jit(solution)/shard_map/all_gather | solution.py:100
Sparse Core Ops, SparseCore 0:
  182.9 554.3 all-reduce.2
  894.0 79.4 all-gather.4
  975.8 121.4 all-gather.6
  1099.3 42.2 all-gather.8
where the time goes:
time: 1150 us
  waiting for transfers between devices  786 us (68%)
  blocking collectives  302 us (26%)
  matrix products  21.1 us (2%)
  starting transfers between devices  17.1 us (1%)
  between operations  13.9 us (1%)
    psum x1, waiting for transfers between devices, shards(): pre_gate, pre_up, hid_grad = lax.psum((gate_part, up_part, hid_part), 'tp')  555 us
    psum x1, blocking collectives, shards(): square = lax.psum(jnp.sum(stream * stream, axis=0), 'tp')  150 us
    psum x1, blocking collectives, shards(): dots = lax.psum(jnp.sum(scaled * normed, axis=0), 'tp')  142 us
    all_gather x1, waiting for transfers between devices, shards(): lax.all_gather(w_out, 'ep', axis=0, tiled=True)  107 us
    all_gather x1, waiting for transfers between devices, shards(): full_grad = lax.all_gather(resid, 'tp', axis=0, tiled=True)  78.9 us
    all_gather x1, waiting for transfers between devices, shards(): ctx_all = lax.all_gather(ctx_local, 'ep', axis=1, tiled=True)  39.3 us
  transfers between devices with their start and end apart: 7, of which 6 were waited for; matrix products, arithmetic and copies ran while one was open for 2% of the time, Pallas kernels for 0%

commit v1 on v0

--- a/solution.py
+++ b/solution.py
@@ -4,6 +4,11 @@
 from jax.sharding import PartitionSpec as P
 
 norm_eps = 1e-06
+
+
+def swapped_in(value, axis, along):
+    stack = jnp.stack([value] * lax.axis_size(axis))
+    return jnp.concatenate(lax.all_to_all(stack, axis, 0, 0), axis=along)
 
 
 def contract_rows(left, right):
@@ -99,7 +104,7 @@
     ctx_local = context[0]
     ctx_all = lax.all_gather(ctx_local, "ep", axis=1, tiled=True)
     weight_sum = contract_cols(grad_block, ctx_all)
-    ctx_total = contract_rows(lax.all_gather(w_out, "ep", axis=0, tiled=True), full_grad)
+    ctx_total = contract_rows(swapped_in(w_out, "ep", 0), full_grad)
     return (
         resid[None],
         ctx_total.astype(jnp.bfloat16)[None],

time: 1150 us -> 1060 us (0.922)
  the two profiles are of different devices: /device:TPU:2 before, /device:TPU:1 now
where the time goes in v1:
time: 1060 us
  waiting for transfers between devices  697 us (66%)
  blocking collectives  296 us (28%)
  matrix products  21.1 us (2%)
  starting transfers between devices  18.6 us (2%)
  between operations  15.6 us (1%)
    psum x1, waiting for transfers between devices, shards(): pre_gate, pre_up, hid_grad = lax.psum((gate_part, up_part, hid_part), 'tp')  561 us
    psum x1, blocking collectives, shards(): square = lax.psum(jnp.sum(stream * stream, axis=0), 'tp')  146 us
    psum x1, blocking collectives, shards(): dots = lax.psum(jnp.sum(scaled * normed, axis=0), 'tp')  141 us
    all_gather x1, waiting for transfers between devices, shards(): full_grad = lax.all_gather(resid, 'tp', axis=0, tiled=True)  76.3 us
    all_gather x1, waiting for transfers between devices, shards(): ctx_all = lax.all_gather(ctx_local, 'ep', axis=1, tiled=True)  48.1 us
  transfers between devices with their start and end apart: 7, of which 6 were waited for; matrix products, arithmetic and copies ran while one was open for 2% of the time, Pallas kernels for 0%

profile of v1, /device:TPU:1, one launch (start us, length us, event | category | flops | bytes accessed | tf_op | source)
XLA Modules:
  0.0 1062.5 jit_solution(11103021335114148634)
XLA Ops:
  8.0 0.0 copy-start
  8.0 0.9 fusion.32
  8.9 145.8 %psum.35 = f32[256]{0:T(256)S(1)} all-reduce(f32[256]{0:T(256)S(1)} %fusion.32), channel_id=1, replica_groups=mesh['tp'=64,'ep'=8] {'tp'}, use_global_device_ids=true, to_apply=%region_1.0 | all-reduce | flops 256 | bytes 2048 | tf_op jit(solution)/shard_map/psum | solution.py:55
  154.7 0.7 iota_compare_fusion.1
  155.5 1.6 fusion.9
  157.1 4.9 all-to-all-start.1
  162.1 1.6 fusion.11
  163.7 3.4 all-to-all-done.1
  167.1 3.3 all-to-all-start
  170.5 0.0 copy-start.1
  170.5 0.0 all-reduce.3.cloned.1.call-start
  170.5 0.0 copy-done
  170.5 1.0 fusion.16
  171.6 2.1 fusion.19
  173.7 1.8 all-to-all-done
  175.5 2.0 fusion.21
  177.5 0.0 all-reduce.3.cloned.1.call-update
  177.5 0.0 all-gather.4.cloned.1.call-start
  177.6 560.9 %all-reduce.3.cloned.1.call-done = (f32[64,2048]{1,0:T(8,128)}, f32[64,2048]{1,0:T(8,128)}, f32[64,2048]{1,0:T(8,128)}) async-done(((f32[64,2048]{1,0:T(8,128)}, f32[64,2048]{1,0:T(8,128)}, f32[64,2048]{1,0:T(8,128)}), (f32[64,2048]{1,0:T(8,128)}, f32[64,2048]{1,0:T(8,128)}, f32[64,2048]{1,0:T(8,128)})) %all-reduce.3.cloned.1.call-update) | async-done | bytes 1572880 | tf_op jit(solution)/shard_map/psum | solution.py:83
  738.5 1.6 multiply_convert_fusion.1
  740.1 0.3 fusion.14
  740.4 0.3 fusion.10
  740.7 0.5 broadcast.38
  741.2 0.7 reduce
  742.0 0.1 reshape.59
  742.1 9.0 all_to_all.72
  751.1 0.1 reshape.60
  751.2 0.3 fusion.27
  751.5 140.7 %psum.39 = f32[256]{0:T(256)S(1)} all-reduce(f32[256]{0:T(256)S(1)} %get-tuple-element.35), channel_id=1, replica_groups=mesh['tp'=64,'ep'=8] {'tp'}, use_global_device_ids=true, to_apply=%region_6.0 | all-reduce | flops 256 | bytes 2048 | tf_op jit(solution)/shard_map/psum | solution.py:98
  892.2 0.7 fusion.31
  892.8 0.0 all-gather.4.cloned.1.call-update
  892.8 2.1 stack.2
  895.0 4.5 all-to-all-start.3
  899.5 76.3 %all-gather.4.cloned.1.call-done = bf16[7168,256]{1,0:T(8,128)(2,1)} async-done(((bf16[112,256]{1,0:T(8,128)(2,1)}), bf16[7168,256]{1,0:T(8,128)(2,1)}) %all-gather.4.cloned.1.call-update) | async-done | bytes 3670032 | tf_op jit(solution)/shard_map/all_gather | solution.py:102
  975.7 6.2 copy.32
  982.0 0.0 all-to-all-done.3
  982.0 5.7 all-to-all-start.4
  987.7 0.0 all-gather.6.cloned.1.call-start
  987.7 0.5 all-gather.6.cloned.1.call-update
  988.3 1.1 fusion
  989.3 1.1 fusion.1
  990.4 0.0 copy-done.2
  990.4 1.1 fusion.2
  991.5 4.3 fusion.3
  995.8 0.8 copy.33
  996.6 48.1 %all-gather.6.cloned.1.call-done = bf16[1,256,2048]{2,1,0:T(8,128)(2,1)} async-done(((bf16[1,256,256]{2,1,0:T(8,128)(2,1)}), bf16[1,256,2048]{2,1,0:T(8,128)(2,1)}) %all-gather.6.cloned.1.call-update) | async-done | bytes 1048592 | tf_op jit(solution)/shard_map/all_gather | solution.py:105
  1044.7 6.2 all-to-all-done.4
  1050.8 4.3 convolution_convert_fusion.3
  (17 shorter events, 0.1 us)
Async XLA Ops:
  8.0 162.5 %copy-start = (bf16[1,112,2048]{2,1,0:T(8,128)(2,1)S(1)}, bf16[1,112,2048]{2,1,0:T(8,128)(2,1)}, u32[]{:S(2)}) copy-start(bf16[1,112,2048]{2,1,0:T(8,128)(2,1)} %param.16) | copy-start | bytes 1376260
  157.1 10.0 all-to-all-start.1
  167.1 8.3 all-to-all-start
  170.5 569.9 %copy-start.1 = (bf16[1,112,2048]{2,1,0:T(8,128)(2,1)S(1)}, bf16[1,112,2048]{2,1,0:T(8,128)(2,1)}, u32[]{:S(2)}) copy-start(bf16[1,112,2048]{2,1,0:T(8,128)(2,1)} %param.17) | copy-start | bytes 1376260
  170.5 568.0 %all-reduce.3.cloned.1.call-start = ((), (), s32[]{:S(2)}) async-start(), calls=%async_computation.7 | async-start | bytes 3145728 | tf_op jit(solution)/shard_map/psum | solution.py:83
  171.6 579.6 %copy-start.5 = (bf16[1,112,256]{2,1,0:T(8,128)(2,1)S(1)}, bf16[1,112,256]{2,1,0:T(8,128)(2,1)}, u32[]{:S(2)}) copy-start(bf16[1,112,256]{2,1,0:T(8,128)(2,1)} %param.11) | copy-start | bytes 172036
  171.6 579.6 %copy-start.7 = (s32[1,8,8]{2,1,0:T(8,128)S(1)}, s32[1,8,8]{2,1,0:T(8,128)}, u32[]{:S(2)}) copy-start(s32[1,8,8]{2,1,0:T(8,128)} %param.19) | copy-start | bytes 772
  171.6 579.6 %copy-start.8 = (f32[112]{0:T(128)S(1)}, f32[112]{0:T(128)}, u32[]{:S(2)}) copy-start(f32[112]{0:T(128)} %param.13) | copy-start | bytes 1348
  171.6 720.6 %copy-start.6 = (bf16[1,112,256]{2,1,0:T(8,128)(2,1)S(1)}, bf16[1,112,256]{2,1,0:T(8,128)(2,1)}, u32[]{:S(2)}) copy-start(bf16[1,112,256]{2,1,0:T(8,128)(2,1)} %param.12) | copy-start | bytes 172036
  173.7 719.2 %copy-start.4 = (bf16[896,256]{1,0:T(8,128)(2,1)S(1)}, bf16[896,256]{1,0:T(8,128)(2,1)}, u32[]{:S(2)}) copy-start(bf16[896,256]{1,0:T(8,128)(2,1)} %param.15) | copy-start | bytes 1376260
  177.5 798.2 %all-gather.4.cloned.1.call-start = ((), (), s32[]{:S(2)}) async-start(), calls=%async_computation.5 | async-start | bytes 3727360 | tf_op jit(solution)/shard_map/all_gather | solution.py:102
  895.0 87.0 %all-to-all-start.3 = ((bf16[8,896,256]{2,1,0:T(8,128)(2,1)}), bf16[8,896,256]{2,1,0:T(8,128)(2,1)}, u32[]{:S(2)}, u32[]{:S(2)}) async-start(bf16[8,896,256]{2,1,0:T(8,128)(2,1)} %stack.2), calls=%async_computation.3 | async-start | bytes 7340032 | tf_op jit(solution)/shard_map/all_to_all | solution.py:11
  982.0 8.4 copy-start.2
  982.0 8.4 copy-start.3
  982.0 68.9 %all-to-all-start.4 = ((bf16[8,896,256]{1,2,0:T(8,128)(2,1)}), bf16[8,896,256]{1,2,0:T(8,128)(2,1)}, u32[]{:S(2)}, u32[]{:S(2)}) async-start(bf16[8,896,256]{1,2,0:T(8,128)(2,1)} %copy.32), calls=%async_computation.4 | async-start | bytes 7340032 | tf_op jit(solution)/shard_map/all_to_all | solution.py:103
  987.7 57.0 %all-gather.6.cloned.1.call-start = ((), (), s32[]{:S(2)}) async-start(), calls=%async_computation.6 | async-start | bytes 1179648 | tf_op jit(solution)/shard_map/all_gather | solution.py:105
Sparse Core Ops, SparseCore 0:
  177.7 560.7 all-reduce.2
  893.0 82.7 all-gather.3
Sparse Core Ops, SparseCore 1:
  990.3 54.3 all-gather.5
